TPU v7x, 128 devices: a whole 4x4x4 slice. The times are simulated.
128 devices in a mesh: tx: 4 (over z), ty: 32 (over x, y, core).
Axes of the slice: x: 4, y: 4, z: 4, core: 2. Of those that a mesh axis runs over, the one named last changes fastest.
Arguments:
- points: bfloat16 [128, 1024, 256], P(('tx', 'ty')), may hold values from -6 to 6
- counts: int32 [128], P(('tx', 'ty')), may hold values from 512 to 1024, as said below
- owner: int32 [128, 1024], P(('tx', 'ty')), may hold values from 0 to 127, as said below
- zorder: int32 [128, 2048], P(('tx', 'ty')), may hold values from 0 to 2047, as said below
- border: int32 [128, 4, 64], P(('tx', 'ty')), may hold values from 0 to 1023, as said below
- near: int32 [128, 16, 1024], P(('tx', 'ty')), may hold values from 0 to 1279, as said below
- w_near: bfloat16 [256, 256], replicated, may hold values from -0.375 to 0.375
- gain_one: float32 [256], replicated, may hold values from 0.1 to 1.9
- conv_w: bfloat16 [3, 8, 32, 32], replicated, may hold values from -0.625 to 0.625
- gain_two: float32 [256], replicated, may hold values from 0.1 to 1.9
- w_up: bfloat16 [256, 1024], replicated, may hold values from -0.375 to 0.375
- w_down: bfloat16 [1024, 256], replicated, may hold values from -0.1875 to 0.1875
- grad_out: bfloat16 [128, 1024, 256], P(('tx', 'ty')), may hold values from -6 to 6
Outputs:
- out_rows: bfloat16 [128, 1024, 256], P(('tx', 'ty'))
- grad_points: bfloat16 [128, 1024, 256], P(('tx', 'ty'))
- grad_w_near: float32 [256, 256], replicated
- grad_gain_one: float32 [256], replicated
- grad_conv: float32 [3, 8, 32, 32], replicated
- grad_gain_two: float32 [256], replicated
- grad_w_up: float32 [256, 1024], replicated
- grad_w_down: float32 [1024, 256], replicated
Inputs may be any that keep to these rules, and one draw needn't show every extreme that they name: `counts`: every tile has at least half of its slots live, and some tile has all of them live. Only live rows count. Among the live rows of one tile at most 16 name the same owner. One particular owner receives exactly 16 live rows from every tile; every other owner receives at most 16 live rows from each tile, so its receive buffer may be partly empty. `zorder`: each owner's entry is a permutation of its 2048 receive slots whose first entries name exactly the filled slots. `border`: each list names distinct live rows of its tile; lists toward a side outside the grid are never read. `near`: indices below 1024 name live rows of the tile; the others name halo rows of blocks whose neighbour tile exists.
All inputs are finite; a program needn't handle non-finite values.
Results may differ from a plain program's by a relative error of at most 0.015.
Values may be sent and summed in bfloat16 or wider, within the bound.
A program may use at most 64 MiB of HBM per device.

v0:
```python
import math
import jax
import jax.numpy as jnp
from jax import lax
from jax.sharding import PartitionSpec as P

PATCH = 1024
eps_norm = 1e-06
gelu_coef = 0.7978845608028654
cubic_coef = 0.044715


def shifted(value, axis, steps):
    count = lax.axis_size(axis)
    initial, last = (max(0, -steps), min(count, count - steps))
    return lax.ppermute(value, axis, [(source, source + steps) for source in range(initial, last)])


def gelu_tanh(value):
    inner = gelu_coef * (value + cubic_coef * value * value * value)
    return 0.5 * value * (1.0 + jnp.tanh(inner))


def gelu_slope(value):
    inner = gelu_coef * (value + cubic_coef * value * value * value)
    tangent = jnp.tanh(inner)
    return 0.5 * (1.0 + tangent) + 0.5 * value * (1.0 - tangent * tangent) * gelu_coef * (
        1.0 + 3.0 * cubic_coef * value * value
    )


def inverse_rms(value):
    return lax.rsqrt(jnp.mean(value * value, axis=-1, keepdims=True) + eps_norm)


def tile_forward(points_tile, halo_rows, near_tile, w_near):
    extended = jnp.concatenate([points_tile, halo_rows], axis=0)
    count_near = near_tile.shape[0]

    def add_neighbour(index, total):
        return total + jnp.take(extended, near_tile[index], axis=0).astype(jnp.float32)

    total = lax.fori_loop(0, count_near, add_neighbour, jnp.zeros(points_tile.shape, jnp.float32))
    average = (total * (1.0 / count_near)).astype(jnp.bfloat16)
    linear_part = jnp.dot(average, w_near, preferred_element_type=jnp.float32)
    lifted = (points_tile.astype(jnp.float32) + gelu_tanh(linear_part)).astype(jnp.bfloat16)
    return (average, linear_part, lifted)


def tile_backward(lifted_grad, average, linear_part, near_tile, w_near, ext_count):
    count_near = near_tile.shape[0]
    tile_rows = lifted_grad.shape[0]
    act_grad = (lifted_grad.astype(jnp.float32) * gelu_slope(linear_part)).astype(jnp.bfloat16)
    near_grad = lax.dot_general(
        average, act_grad, (((0,), (0,)), ((), ())), preferred_element_type=jnp.float32
    )
    spread = lax.dot_general(
        act_grad, w_near, (((1,), (1,)), ((), ())), preferred_element_type=jnp.float32
    ) * (1.0 / count_near)

    def scatter_neighbour(index, total):
        return total.at[near_tile[index]].add(spread)

    ext_grad = lax.fori_loop(
        0, count_near, scatter_neighbour, jnp.zeros((ext_count, spread.shape[1]), jnp.float32)
    )
    row_grad = lifted_grad.astype(jnp.float32) + ext_grad[:tile_rows]
    halo_grad = ext_grad[tile_rows:].astype(jnp.bfloat16)
    return (near_grad, row_grad, halo_grad)


def route_ranks(owner_tile, count, tiles):
    tile_rows = owner_tile.shape[0]
    index = jnp.arange(tile_rows, dtype=jnp.int32)
    live = index < count
    score = jnp.where(live, owner_tile * tile_rows + index, tiles * tile_rows + index)
    order = jnp.argsort(score, stable=True)
    members = (owner_tile[:, None] == jnp.arange(tiles, dtype=jnp.int32)[None, :]) & live[:, None]
    per_owner = jnp.sum(members.astype(jnp.int32), axis=0)
    starts = jnp.cumsum(per_owner) - per_owner
    sorted_owner = jnp.take(owner_tile, order)
    ranked = index - jnp.take(starts, sorted_owner)
    rank = jnp.zeros((tile_rows,), jnp.int32).at[order].set(ranked)
    return (rank, live)


def shift_down(rows):
    return jnp.concatenate([jnp.zeros_like(rows[:1]), rows[:-1]], axis=0)


def shift_up(rows):
    return jnp.concatenate([rows[1:], jnp.zeros_like(rows[:1])], axis=0)


def block_taps(conv_w):
    groups, inner = (conv_w.shape[1], conv_w.shape[2])
    identity_blocks = jnp.eye(groups, dtype=conv_w.dtype)
    full = jnp.einsum("gh,ogab->ogahb", identity_blocks, conv_w)
    return full.reshape(conv_w.shape[0], groups * inner, groups * inner)


def grouped_weight(inputs, outputs, groups, inner):
    length = inputs.shape[0]
    left = inputs.reshape(length, groups, inner)
    right = outputs.reshape(length, groups, inner)
    return jnp.einsum("pga,pgb->gab", left, right, preferred_element_type=jnp.float32)


def tap_back(rows, tap):
    return lax.dot_general(rows, tap, (((1,), (1,)), ((), ())), preferred_element_type=jnp.float32)


def patch_pass(serial, out_grad, gain_one, conv_w, taps_full, gain_two, w_up, w_down):
    groups, inner = (conv_w.shape[1], conv_w.shape[2])
    serial_f = serial.astype(jnp.float32)
    scale_one = inverse_rms(serial_f)
    normed = (serial_f * scale_one * gain_one).astype(jnp.bfloat16)
    taps = (shift_down(normed), normed, shift_up(normed))
    mixed = (
        jnp.dot(taps[0], taps_full[0], preferred_element_type=jnp.float32)
        + jnp.dot(taps[1], taps_full[1], preferred_element_type=jnp.float32)
        + jnp.dot(taps[2], taps_full[2], preferred_element_type=jnp.float32)
    )
    state = serial_f + mixed
    scale_two = inverse_rms(state)
    second = (state * scale_two * gain_two).astype(jnp.bfloat16)
    hidden_pre = jnp.dot(second, w_up, preferred_element_type=jnp.float32)
    hidden = gelu_tanh(hidden_pre).astype(jnp.bfloat16)
    result = (state + jnp.dot(hidden, w_down, preferred_element_type=jnp.float32)).astype(
        jnp.bfloat16
    )
    down_grad = lax.dot_general(
        hidden, out_grad, (((0,), (0,)), ((), ())), preferred_element_type=jnp.float32
    )
    hidden_grad = lax.dot_general(
        out_grad, w_down, (((1,), (1,)), ((), ())), preferred_element_type=jnp.float32
    ).astype(jnp.bfloat16)
    pre_grad = (hidden_grad.astype(jnp.float32) * gelu_slope(hidden_pre)).astype(jnp.bfloat16)
    up_grad = lax.dot_general(
        second, pre_grad, (((0,), (0,)), ((), ())), preferred_element_type=jnp.float32
    )
    second_grad = lax.dot_general(
        pre_grad, w_up, (((1,), (1,)), ((), ())), preferred_element_type=jnp.float32
    ).astype(jnp.bfloat16)
    unit_two = state * scale_two
    weighted_two = second_grad.astype(jnp.float32) * gain_two
    gain_two_grad = jnp.sum(second_grad.astype(jnp.float32) * unit_two, axis=0)
    state_grad = out_grad.astype(jnp.float32) + scale_two * (
        weighted_two - unit_two * jnp.mean(weighted_two * unit_two, axis=-1, keepdims=True)
    )
    mixed_grad = state_grad.astype(jnp.bfloat16)
    conv_grad = jnp.stack(
        [
            grouped_weight(taps[0], mixed_grad, groups, inner),
            grouped_weight(taps[1], mixed_grad, groups, inner),
            grouped_weight(taps[2], mixed_grad, groups, inner),
        ],
        axis=0,
    )
    normed_grad = (
        shift_up(tap_back(mixed_grad, taps_full[0]))
        + tap_back(mixed_grad, taps_full[1])
        + shift_down(tap_back(mixed_grad, taps_full[2]))
    ).astype(jnp.bfloat16)
    unit_one = serial_f * scale_one
    weighted_one = normed_grad.astype(jnp.float32) * gain_one
    gain_one_grad = jnp.sum(normed_grad.astype(jnp.float32) * unit_one, axis=0)
    serial_grad = (
        state_grad
        + scale_one
        * (weighted_one - unit_one * jnp.mean(weighted_one * unit_one, axis=-1, keepdims=True))
    ).astype(jnp.bfloat16)
    return (result, serial_grad, (gain_one_grad, conv_grad, gain_two_grad, up_grad, down_grad))


def pass_columns(rows, shift_by):
    return shifted(rows, "tx", shift_by)


def pass_lines(rows, shift_by):
    return shifted(rows, "ty", shift_by)


def body(
    points,
    counts,
    owner,
    zorder,
    border,
    near,
    w_near,
    gain_one,
    conv_w,
    gain_two,
    w_up,
    w_down,
    grad_out,
):
    points_tile = points[0]
    tile_rows, width = points_tile.shape
    lists = border[0]
    border_rows = lists.shape[1]
    cols_count = lax.axis_size("tx")
    lines_count = lax.axis_size("ty")
    tiles = cols_count * lines_count
    recv_rows = zorder.shape[1]
    capacity = recv_rows // tiles
    near_tile = near[0]
    owner_tile = owner[0]
    sent = jnp.take(points_tile, lists.reshape(-1), axis=0).reshape(4, border_rows, width)
    halo = jnp.concatenate(
        [
            pass_columns(sent[0], -1),
            pass_columns(sent[1], 1),
            pass_lines(sent[2], -1),
            pass_lines(sent[3], 1),
        ],
        axis=0,
    )
    average, linear_part, lifted = tile_forward(points_tile, halo, near_tile, w_near)
    rank, live = route_ranks(owner_tile, counts[0], tiles)
    slots = jnp.where(live, owner_tile * capacity + rank, tiles * capacity)
    payload = jnp.concatenate([lifted, grad_out[0]], axis=1)
    outgoing = (
        jnp.zeros((tiles * capacity, 2 * width), jnp.bfloat16).at[slots].set(payload, mode="drop")
    )
    incoming = lax.all_to_all(outgoing, ("tx", "ty"), split_axis=0, concat_axis=0, tiled=True)
    serial_both = jnp.take(incoming, zorder[0], axis=0)
    taps_full = block_taps(conv_w)
    zero_sums = (
        jnp.zeros((width,), jnp.float32),
        jnp.zeros(conv_w.shape, jnp.float32),
        jnp.zeros((width,), jnp.float32),
        jnp.zeros(w_up.shape, jnp.float32),
        jnp.zeros(w_down.shape, jnp.float32),
    )

    def patch_step(carry, block):
        result, serial_grad, grads = patch_pass(
            block[:, :width], block[:, width:], gain_one, conv_w, taps_full, gain_two, w_up, w_down
        )
        return (jax.tree.map(lambda left, right: left + right, carry, grads), (result, serial_grad))

    sums, (results, serial_grads) = lax.scan(
        patch_step, zero_sums, serial_both.reshape(recv_rows // PATCH, PATCH, 2 * width)
    )
    back = jnp.concatenate(
        [results.reshape(recv_rows, width), serial_grads.reshape(recv_rows, width)], axis=1
    )
    back_slots = jnp.zeros_like(back).at[zorder[0]].set(back)
    returned = lax.all_to_all(back_slots, ("tx", "ty"), split_axis=0, concat_axis=0, tiled=True)
    back_rows = jnp.take(returned, slots, axis=0, mode="fill", fill_value=0)
    out_rows = back_rows[:, :width]
    lifted_grad = back_rows[:, width:]
    near_grad, row_grad, halo_grad = tile_backward(
        lifted_grad, average, linear_part, near_tile, w_near, tile_rows + 4 * border_rows
    )
    came_back = (
        pass_columns(halo_grad[0:border_rows], 1),
        pass_columns(halo_grad[border_rows : 2 * border_rows], -1),
        pass_lines(halo_grad[2 * border_rows : 3 * border_rows], 1),
        pass_lines(halo_grad[3 * border_rows : 4 * border_rows], -1),
    )
    for direction in range(4):
        row_grad = row_grad.at[lists[direction]].add(came_back[direction].astype(jnp.float32))
    near_sum, gain_one_sum, conv_sum, gain_two_sum, up_sum, down_sum = lax.psum(
        (near_grad, sums[0], sums[1], sums[2], sums[3], sums[4]), ("tx", "ty")
    )
    totals = (gain_one_sum, conv_sum, gain_two_sum, up_sum, down_sum)
    scale = 1.0 / math.sqrt(tiles * tile_rows)
    return (
        out_rows[None],
        row_grad.astype(jnp.bfloat16)[None],
        near_sum * scale,
        totals[0] * scale,
        totals[1] * scale,
        totals[2] * scale,
        totals[3] * scale,
        totals[4] * scale,
    )


def solution(mesh):
    placed = (
        P(("tx", "ty"), None, None),
        P(("tx", "ty")),
        P(("tx", "ty"), None),
        P(("tx", "ty"), None),
        P(("tx", "ty"), None, None),
        P(("tx", "ty"), None, None),
        P(),
        P(),
        P(),
        P(),
        P(),
        P(),
        P(("tx", "ty"), None, None),
    )
    return jax.shard_map(
        body,
        mesh=mesh,
        in_specs=placed,
        out_specs=(
            P(("tx", "ty"), None, None),
            P(("tx", "ty"), None, None),
            P(),
            P(),
            P(),
            P(),
            P(),
            P(),
        ),
        check_vma=False,
    )
```

profile of v0, /device:TPU:1, one launch (start us, length us, event | category | flops | bytes accessed | tf_op | source)
XLA Modules:
  0.0 547.0 jit_solution(10170970694803453524)
XLA Ops:
  11.1 4.6 collective-permute-start.3
  17.6 3.5 collective-permute-start.1
  24.9 4.4 sort.17
  29.3 4.5 gather_fusion.1
  34.2 6.6 %gather_fusion.2 = s32[1024]{0:T(1024)S(1)} fusion(s32[128]{0:T(128)S(1)} %sub.18, s32[1024]{0:T(1024)S(1)} %broadcast_clamp_fusion.3), kind=kCustom, calls=%fused_computation.2 | custom fusion | bytes 12288 | tf_op jit(solution)/shard_map/jit(_take)/gather | solution.py:82
  40.8 4.3 scatter_custom_fusion.1
  49.6 81.9 %while.51 = (s32[]{:T(128)}, f32[1024,256]{1,0:T(8,128)S(1)}, s32[16,1024]{1,0:T(8,128)}, bf16[1280,256]{1,0:T(8,128)(2,1)S(1)}, s32[]{:T(128)}, /*index=5*/s32[]{:T(128)}) while((s32[]{:T(128)}, f32[1024,256]{1,0:T(8,128)S(1)}, s32[16,1024]{1,0:T(8,128)}, bf16[1280,256]{1,0:T(8,128)(2,1)S(1)}, s32[]{:T(128)}, ...), condition=%wide.region_5.6_spmd.clone, body=%wide.region_4.5_spmd.clone.sunk | while | flops 1058819 | bytes 3700827 | solution.py:43
  50.5 3.9 gather_fusion
  55.6 3.9 gather_fusion
  60.7 3.9 gather_fusion
  65.8 3.9 gather_fusion
  70.9 3.9 gather_fusion
  76.0 3.9 gather_fusion
  81.2 3.9 gather_fusion
  86.3 3.9 gather_fusion
  91.4 3.9 gather_fusion
  96.5 3.9 gather_fusion
  101.6 3.9 gather_fusion
  106.7 3.9 gather_fusion
  111.9 3.9 gather_fusion
  117.0 3.9 gather_fusion
  122.1 3.9 gather_fusion
  127.2 3.9 gather_fusion
  133.7 6.7 %scatter_custom_fusion.2 = bf16[2048,512]{1,0:T(8,128)(2,1)} fusion(s32[1024]{0:T(1024)S(1)} %get-tuple-element.408, bf16[1024,512]{1,0:T(8,128)(2,1)S(1)} %copy.65, bf16[]{:T(256)} %constant.215.clone.1), kind=kCustom, calls=%fused_computation.126 | custom fusion | bytes 2097154 | tf_op jit(solution)/shard_map/scatter | solution.py:225
  140.4 22.0 %all-to-all-start = ((bf16[128,16,512]{2,1,0:T(8,128)(2,1)}), bf16[128,16,512]{2,1,0:T(8,128)(2,1)S(1)}, u32[]{:S(2)}, u32[]{:S(2)}) async-start(bf16[128,16,512]{2,1,0:T(8,128)(2,1)} %bitcast.194), calls=%async_computation | async-start | bytes 4194304 | tf_op jit(solution)/shard_map/all_to_all | solution.py:227
  163.7 2.3 multiply_bitcast_fusion
  166.0 3.0 reshape.393
  169.1 23.7 %all-to-all-done = bf16[128,16,512]{2,1,0:T(8,128)(2,1)S(1)} async-done(((bf16[128,16,512]{2,1,0:T(8,128)(2,1)}), bf16[128,16,512]{2,1,0:T(8,128)(2,1)S(1)}, u32[]{:S(2)}, u32[]{:S(2)}) %all-to-all-start) | async-done | bytes 2097184 | tf_op jit(solution)/shard_map/all_to_all | solution.py:227
  192.8 9.2 %gather_fusion.4 = bf16[2048,512]{1,0:T(8,128)(2,1)} fusion(bf16[2048,512]{1,0:T(8,128)(2,1)S(1)} %bitcast.188, s32[2048]{0:T(1024)S(1)} %broadcast_clamp_fusion.1), kind=kCustom, calls=%fused_computation.4 | custom fusion | bytes 4202496 | tf_op jit(solution)/shard_map/jit(_take)/gather | solution.py:228
  202.0 3.0 copy.66
  206.6 68.3 %while.52 = (s32[]{:T(128)}, f32[256]{0:T(256)S(1)}, f32[3,8,32,32]{3,2,1,0:T(8,128)}, f32[256]{0:T(256)S(1)}, f32[256,1024]{1,0:T(8,128)}, /*index=5*/f32[1024,...) while((s32[]{:T(128)}, f32[256]{0:T(256)S(1)}, ...), condition=%wide.region_14.15_spmd.clone, body=%wide.region_7.14_spmd.clone.sunk | while | flops 4135946752 | bytes 123703776 | solution.py:244
  218.0 2.5 fusion.180
  221.8 4.9 convolution_add_fusion.11
  226.7 3.0 fusion.173
  252.0 2.5 fusion.180
  255.8 5.2 convolution_add_fusion.11
  261.0 3.0 fusion.173
  274.9 11.5 %scatter_custom_fusion.3 = bf16[2048,512]{1,0:T(8,128)(2,1)} fusion(s32[2048]{0:T(1024)} %bitcast.205, bf16[2048,256]{1,0:T(8,128)(2,1)} %bitcast.198, bf16[]{:T(256)} %constant.244, bf16[2048,256]{1,0:T(8,128)(2,1)} %bitcast.199, bf16[]{:T(256)} %constant.215.clone.1), kind=kCustom, calls=%fused_computation.105 | custom fusion | flops 4194304 | bytes 4195328 | tf_op jit(solution)/shard_map/scatter | solution.py:250
  286.4 4.3 all-to-all-start.1
  291.3 81.3 %all-reduce.4 = (f32[256]{0:T(256)S(1)}, f32[256]{0:T(256)S(1)}) all-reduce(f32[256]{0:T(256)S(1)} %get-tuple-element.250, f32[256]{0:T(256)S(1)} %get-tuple-element.252), channel_id=1, replica_groups=mesh['tx'=4,'ty'=32] {'tx','ty'}, use_global_device_ids=true, to_apply=%region_24.25 | all-reduce | flops 512 | bytes 4096 | tf_op jit(solution)/shard_map/psum | solution.py:266
  373.2 4.0 gather_fusion.5
  381.2 117.5 %while.50 = (s32[]{:T(128)}, f32[1280,256]{1,0:T(8,128)S(1)}, s32[16,1024]{1,0:T(8,128)}, f32[1024,256]{1,0:T(8,128)S(1)}, s32[]{:T(128)}) while((s32[]{:T(128)}, f32[1280,256]{1,0:T(8,128)S(1)}, s32[16,1024]{1,0:T(8,128)}, f32[1024,256]{1,0:T(8,128)S(1)}, s32[]{:T(128)}) %tuple.124), condition=%wide.region_18.19_spmd, body=%wide.region_16.18_spmd.sunk | while | flops 265218 | bytes 3158089 | solution.py:64
  382.0 6.5 %scatter_fusion = f32[1280,256]{1,0:T(8,128)S(1)} fusion(f32[1280,256]{1,0:T(8,128)S(1)} %get-tuple-element.679, s32[1024]{0:T(1024)S(1)} %bitcast.200, f32[1024,256]{1,0:T(8,128)S(1)} %get-tuple-element.686), kind=kCustom, calls=%fused_computation.6.clone.1 | custom fusion | flops 262144 | bytes 3149824 | tf_op jit(solution)/shard_map/while/body/eval_jaxpr/scatter-add | solution.py:62
  389.4 6.5 %scatter_fusion = f32[1280,256]{1,0:T(8,128)S(1)} fusion(f32[1280,256]{1,0:T(8,128)S(1)} %get-tuple-element.679, s32[1024]{0:T(1024)S(1)} %bitcast.200, f32[1024,256]{1,0:T(8,128)S(1)} %get-tuple-element.686), kind=kCustom, calls=%fused_computation.6.clone.1 | custom fusion | flops 262144 | bytes 3149824 | tf_op jit(solution)/shard_map/while/body/eval_jaxpr/scatter-add | solution.py:62
  396.7 6.5 %scatter_fusion = f32[1280,256]{1,0:T(8,128)S(1)} fusion(f32[1280,256]{1,0:T(8,128)S(1)} %get-tuple-element.679, s32[1024]{0:T(1024)S(1)} %bitcast.200, f32[1024,256]{1,0:T(8,128)S(1)} %get-tuple-element.686), kind=kCustom, calls=%fused_computation.6.clone.1 | custom fusion | flops 262144 | bytes 3149824 | tf_op jit(solution)/shard_map/while/body/eval_jaxpr/scatter-add | solution.py:62
  404.1 6.5 %scatter_fusion = f32[1280,256]{1,0:T(8,128)S(1)} fusion(f32[1280,256]{1,0:T(8,128)S(1)} %get-tuple-element.679, s32[1024]{0:T(1024)S(1)} %bitcast.200, f32[1024,256]{1,0:T(8,128)S(1)} %get-tuple-element.686), kind=kCustom, calls=%fused_computation.6.clone.1 | custom fusion | flops 262144 | bytes 3149824 | tf_op jit(solution)/shard_map/while/body/eval_jaxpr/scatter-add | solution.py:62
  411.4 6.5 %scatter_fusion = f32[1280,256]{1,0:T(8,128)S(1)} fusion(f32[1280,256]{1,0:T(8,128)S(1)} %get-tuple-element.679, s32[1024]{0:T(1024)S(1)} %bitcast.200, f32[1024,256]{1,0:T(8,128)S(1)} %get-tuple-element.686), kind=kCustom, calls=%fused_computation.6.clone.1 | custom fusion | flops 262144 | bytes 3149824 | tf_op jit(solution)/shard_map/while/body/eval_jaxpr/scatter-add | solution.py:62
  418.7 6.5 %scatter_fusion = f32[1280,256]{1,0:T(8,128)S(1)} fusion(f32[1280,256]{1,0:T(8,128)S(1)} %get-tuple-element.679, s32[1024]{0:T(1024)S(1)} %bitcast.200, f32[1024,256]{1,0:T(8,128)S(1)} %get-tuple-element.686), kind=kCustom, calls=%fused_computation.6.clone.1 | custom fusion | flops 262144 | bytes 3149824 | tf_op jit(solution)/shard_map/while/body/eval_jaxpr/scatter-add | solution.py:62
  426.1 6.5 %scatter_fusion = f32[1280,256]{1,0:T(8,128)S(1)} fusion(f32[1280,256]{1,0:T(8,128)S(1)} %get-tuple-element.679, s32[1024]{0:T(1024)S(1)} %bitcast.200, f32[1024,256]{1,0:T(8,128)S(1)} %get-tuple-element.686), kind=kCustom, calls=%fused_computation.6.clone.1 | custom fusion | flops 262144 | bytes 3149824 | tf_op jit(solution)/shard_map/while/body/eval_jaxpr/scatter-add | solution.py:62
  433.4 6.5 %scatter_fusion = f32[1280,256]{1,0:T(8,128)S(1)} fusion(f32[1280,256]{1,0:T(8,128)S(1)} %get-tuple-element.679, s32[1024]{0:T(1024)S(1)} %bitcast.200, f32[1024,256]{1,0:T(8,128)S(1)} %get-tuple-element.686), kind=kCustom, calls=%fused_computation.6.clone.1 | custom fusion | flops 262144 | bytes 3149824 | tf_op jit(solution)/shard_map/while/body/eval_jaxpr/scatter-add | solution.py:62
  440.8 6.5 %scatter_fusion = f32[1280,256]{1,0:T(8,128)S(1)} fusion(f32[1280,256]{1,0:T(8,128)S(1)} %get-tuple-element.679, s32[1024]{0:T(1024)S(1)} %bitcast.200, f32[1024,256]{1,0:T(8,128)S(1)} %get-tuple-element.686), kind=kCustom, calls=%fused_computation.6.clone.1 | custom fusion | flops 262144 | bytes 3149824 | tf_op jit(solution)/shard_map/while/body/eval_jaxpr/scatter-add | solution.py:62
  448.1 6.5 %scatter_fusion = f32[1280,256]{1,0:T(8,128)S(1)} fusion(f32[1280,256]{1,0:T(8,128)S(1)} %get-tuple-element.679, s32[1024]{0:T(1024)S(1)} %bitcast.200, f32[1024,256]{1,0:T(8,128)S(1)} %get-tuple-element.686), kind=kCustom, calls=%fused_computation.6.clone.1 | custom fusion | flops 262144 | bytes 3149824 | tf_op jit(solution)/shard_map/while/body/eval_jaxpr/scatter-add | solution.py:62
  455.5 6.5 %scatter_fusion = f32[1280,256]{1,0:T(8,128)S(1)} fusion(f32[1280,256]{1,0:T(8,128)S(1)} %get-tuple-element.679, s32[1024]{0:T(1024)S(1)} %bitcast.200, f32[1024,256]{1,0:T(8,128)S(1)} %get-tuple-element.686), kind=kCustom, calls=%fused_computation.6.clone.1 | custom fusion | flops 262144 | bytes 3149824 | tf_op jit(solution)/shard_map/while/body/eval_jaxpr/scatter-add | solution.py:62
  462.8 6.5 %scatter_fusion = f32[1280,256]{1,0:T(8,128)S(1)} fusion(f32[1280,256]{1,0:T(8,128)S(1)} %get-tuple-element.679, s32[1024]{0:T(1024)S(1)} %bitcast.200, f32[1024,256]{1,0:T(8,128)S(1)} %get-tuple-element.686), kind=kCustom, calls=%fused_computation.6.clone.1 | custom fusion | flops 262144 | bytes 3149824 | tf_op jit(solution)/shard_map/while/body/eval_jaxpr/scatter-add | solution.py:62
  470.1 6.5 %scatter_fusion = f32[1280,256]{1,0:T(8,128)S(1)} fusion(f32[1280,256]{1,0:T(8,128)S(1)} %get-tuple-element.679, s32[1024]{0:T(1024)S(1)} %bitcast.200, f32[1024,256]{1,0:T(8,128)S(1)} %get-tuple-element.686), kind=kCustom, calls=%fused_computation.6.clone.1 | custom fusion | flops 262144 | bytes 3149824 | tf_op jit(solution)/shard_map/while/body/eval_jaxpr/scatter-add | solution.py:62
  477.5 6.5 %scatter_fusion = f32[1280,256]{1,0:T(8,128)S(1)} fusion(f32[1280,256]{1,0:T(8,128)S(1)} %get-tuple-element.679, s32[1024]{0:T(1024)S(1)} %bitcast.200, f32[1024,256]{1,0:T(8,128)S(1)} %get-tuple-element.686), kind=kCustom, calls=%fused_computation.6.clone.1 | custom fusion | flops 262144 | bytes 3149824 | tf_op jit(solution)/shard_map/while/body/eval_jaxpr/scatter-add | solution.py:62
  484.8 6.5 %scatter_fusion = f32[1280,256]{1,0:T(8,128)S(1)} fusion(f32[1280,256]{1,0:T(8,128)S(1)} %get-tuple-element.679, s32[1024]{0:T(1024)S(1)} %bitcast.200, f32[1024,256]{1,0:T(8,128)S(1)} %get-tuple-element.686), kind=kCustom, calls=%fused_computation.6.clone.1 | custom fusion | flops 262144 | bytes 3149824 | tf_op jit(solution)/shard_map/while/body/eval_jaxpr/scatter-add | solution.py:62
  492.2 6.5 %scatter_fusion = f32[1280,256]{1,0:T(8,128)S(1)} fusion(f32[1280,256]{1,0:T(8,128)S(1)} %get-tuple-element.679, s32[1024]{0:T(1024)S(1)} %bitcast.200, f32[1024,256]{1,0:T(8,128)S(1)} %get-tuple-element.686), kind=kCustom, calls=%fused_computation.6.clone.1 | custom fusion | flops 262144 | bytes 3149824 | tf_op jit(solution)/shard_map/while/body/eval_jaxpr/scatter-add | solution.py:62
  500.3 2.5 collective-permute-start.7
  502.8 3.4 collective-permute-start.6
  507.5 4.0 collective-permute-start.4
  520.6 11.0 %all-reduce.8.cloned.1.call-done = (f32[256,256]{1,0:T(8,128)}, f32[3,8,32,32]{3,2,1,0:T(8,128)}, f32[256,1024]{1,0:T(8,128)}, f32[1024,256]{1,0:T(8,128)}) async-done(((f32[256,256]{1,0:T(8,128)}, f32[3,8,32,32]{3,2,1,0:T(8,128)}, f32[256,1024]{1,0:T(8,128)}, f32[1024,256]{1,0:T(8,128)}), (f32[256,256]{1,0:T(8,128)}, f32[3,8,32,32]{3,2,1,0:T(8,128)}, f32[256,1024]{1,0:T(8,128)}, ...) | async-done | bytes 2457616 | tf_op jit(solution)/shard_map/psum | solution.py:266
  535.1 2.3 broadcast_multiply_fusion.3
  537.5 2.3 broadcast_multiply_fusion.2
  (297 shorter events, 116.2 us)
Async XLA Ops:
  7.2 124.4 %copy-start = (bf16[256,256]{1,0:T(8,128)(2,1)S(1)}, bf16[256,256]{1,0:T(8,128)(2,1)}, u32[]{:S(2)}) copy-start(bf16[256,256]{1,0:T(8,128)(2,1)} %param.25) | copy-start | bytes 393220
  7.2 22.1 %copy-start.1 = (s32[1,1024]{1,0:T(1,128)S(1)}, s32[1,1024]{1,0:T(1,128)}, u32[]{:S(2)}) copy-start(s32[1,1024]{1,0:T(1,128)} %param.21) | copy-start | bytes 12292
  11.1 35.9 %collective-permute-start.3 = (bf16[64,256]{0,1:T(8,128)(2,1)S(1)}, bf16[64,256]{0,1:T(8,128)(2,1)S(1)}, u32[]{:S(2)}, u32[]{:S(2)}) collective-permute-start(bf16[64,256]{0,1:T(8,128)(2,1)S(1)} %get-tuple-element.423), channel_id=1, source_target_pairs={{0,1},{1,2},{2,3},{3,4},{4,5},{5,6},{6,7},{7,8},{8,9},{9,10},{10,1... | collective-permute-start | bytes 98312 | tf_op jit(solution)/shard_map/ppermute | solution.py:16
  15.7 31.3 %collective-permute-start.2 = (bf16[64,256]{0,1:T(8,128)(2,1)S(1)}, bf16[64,256]{0,1:T(8,128)(2,1)S(1)}, u32[]{:S(2)}, u32[]{:S(2)}) collective-permute-start(bf16[64,256]{0,1:T(8,128)(2,1)S(1)} %get-tuple-element.424), channel_id=1, source_target_pairs={{1,0},{2,1},{3,2},{4,3},{5,4},{6,5},{7,6},{8,7},{9,8},{10,9},{11,1... | collective-permute-start | bytes 98312 | tf_op jit(solution)/shard_map/ppermute | solution.py:16
  17.6 29.4 %collective-permute-start.1 = (bf16[64,256]{0,1:T(8,128)(2,1)S(1)}, bf16[64,256]{0,1:T(8,128)(2,1)S(1)}, u32[]{:S(2)}, u32[]{:S(2)}) collective-permute-start(bf16[64,256]{0,1:T(8,128)(2,1)S(1)} %get-tuple-element.425), channel_id=1, source_target_pairs={{0,32},{32,64},{64,96},{1,33},{33,65},{65,97},{2,34},{34,66},{66,9... | collective-permute-start | bytes 98312 | tf_op jit(solution)/shard_map/ppermute | solution.py:16
  21.2 25.8 %collective-permute-start = (bf16[64,256]{0,1:T(8,128)(2,1)S(1)}, bf16[64,256]{0,1:T(8,128)(2,1)S(1)}, u32[]{:S(2)}, u32[]{:S(2)}) collective-permute-start(bf16[64,256]{0,1:T(8,128)(2,1)S(1)} %get-tuple-element.426), channel_id=1, source_target_pairs={{32,0},{64,32},{96,64},{33,1},{65,33},{97,65},{34,2},{66,34},{98,6... | collective-permute-start | bytes 98312 | tf_op jit(solution)/shard_map/ppermute | solution.py:16
  29.3 16.5 %copy-start.12 = (bf16[1,1024,256]{2,1,0:T(8,128)(2,1)S(1)}, bf16[1,1024,256]{2,1,0:T(8,128)(2,1)}, u32[]{:S(2)}) copy-start(bf16[1,1024,256]{2,1,0:T(8,128)(2,1)} %param.19) | copy-start | bytes 1572868
  29.3 16.7 %copy-start.14 = (bf16[1,1024,256]{2,1,0:T(8,128)(2,1)S(1)}, bf16[1,1024,256]{2,1,0:T(8,128)(2,1)}, u32[]{:S(2)}) copy-start(bf16[1,1024,256]{2,1,0:T(8,128)(2,1)} %param.31) | copy-start | bytes 1572868
  45.7 87.9 %copy-start.24 = (s32[1024]{0:T(1024)}, s32[1024]{0:T(1024)S(1)}, u32[]{:S(2)}) copy-start(s32[1024]{0:T(1024)S(1)} %get-tuple-element.408) | copy-start | bytes 12292
  47.0 0.6 copy-start.17
  47.0 0.6 copy-start.18
  47.0 0.6 copy-start.19
  47.7 0.6 copy-start.20
  49.6 83.5 %copy-start.13 = (bf16[1,1024,256]{1,2,0:T(8,128)(2,1)S(1)}, bf16[1,1024,256]{1,2,0:T(8,128)(2,1)}, u32[]{:S(2)}) copy-start(bf16[1,1024,256]{1,2,0:T(8,128)(2,1)} %copy.64) | copy-start | bytes 1572868
  131.5 8.9 %copy-start.6 = (f32[1024,256]{1,0:T(8,128)}, f32[1024,256]{1,0:T(8,128)S(1)}, u32[]{:S(2)}) copy-start(f32[1024,256]{1,0:T(8,128)S(1)} %get-tuple-element.246) | copy-start | bytes 3145732
  133.1 29.9 %copy-start.21 = (s32[1,2048]{1,0:T(1,128)S(1)}, s32[1,2048]{1,0:T(1,128)}, u32[]{:S(2)}) copy-start(s32[1,2048]{1,0:T(1,128)} %param.22) | copy-start | bytes 24580
  140.4 52.4 %all-to-all-start = ((bf16[128,16,512]{2,1,0:T(8,128)(2,1)}), bf16[128,16,512]{2,1,0:T(8,128)(2,1)S(1)}, u32[]{:S(2)}, u32[]{:S(2)}) async-start(bf16[128,16,512]{2,1,0:T(8,128)(2,1)} %bitcast.194), calls=%async_computation | async-start | bytes 4194304 | tf_op jit(solution)/shard_map/all_to_all | solution.py:227
  169.1 32.9 %copy-start.22 = (s32[2048,1]{0,1:T(1,128)}, s32[2048,1]{0,1:T(1,128)S(1)}, u32[]{:S(2)}) copy-start(s32[2048,1]{0,1:T(1,128)S(1)} %compare_select_fusion.3) | copy-start | bytes 24580
  202.0 4.6 copy-start.15
  202.0 4.6 copy-start.16
  213.4 4.7 copy-start.27
  216.1 1.9 copy-start.2
  221.8 4.9 copy-start.3
  221.8 4.9 copy-start.28
  229.8 2.1 copy-start.8
  231.9 1.3 copy-start.4
  231.9 1.9 copy-start.5
  232.8 3.0 copy-start.9
  232.8 1.3 copy-start.10
  234.3 4.3 copy-start.11
  247.4 4.7 copy-start.27
  250.1 1.9 copy-start.2
  255.8 5.2 copy-start.3
  255.8 5.2 copy-start.28
  264.1 2.1 copy-start.8
  266.2 1.3 copy-start.4
  266.2 1.9 copy-start.5
  267.1 3.0 copy-start.9
  267.1 1.3 copy-start.10
  268.6 4.3 copy-start.11
  274.9 15.9 %copy-start.23 = (s32[1,4,64]{2,1,0:T(4,128)S(1)}, s32[1,4,64]{2,1,0:T(4,128)}, u32[]{:S(2)}) copy-start(s32[1,4,64]{2,1,0:T(4,128)} %param.23) | copy-start | bytes 3076
  274.9 16.4 %copy-start.25 = (s32[1024]{0:T(1024)S(1)}, s32[1024]{0:T(1024)}, u32[]{:S(2)}) copy-start(s32[1024]{0:T(1024)} %copy-done.24) | copy-start | bytes 12292
  286.4 86.8 %all-to-all-start.1 = ((bf16[128,16,512]{2,1,0:T(8,128)(2,1)}), bf16[128,16,512]{2,1,0:T(8,128)(2,1)S(1)}, u32[]{:S(2)}, u32[]{:S(2)}) async-start(bf16[128,16,512]{2,1,0:T(8,128)(2,1)} %bitcast.193), calls=%async_computation.1 | async-start | bytes 4194304 | tf_op jit(solution)/shard_map/all_to_all | solution.py:251
  290.7 240.9 %all-reduce.8.cloned.1.call-start = ((), (), s32[]{:S(2)}) async-start(), calls=%async_computation.2 | async-start | bytes 5505024 | tf_op jit(solution)/shard_map/psum | solution.py:266
  373.2 4.5 copy-start.26
  377.1 2.6 copy-start.7
  500.3 18.1 %collective-permute-start.7 = (bf16[64,256]{1,0:T(8,128)(2,1)S(1)}, bf16[64,256]{1,0:T(8,128)(2,1)S(1)}, u32[]{:S(2)}, u32[]{:S(2)}) collective-permute-start(bf16[64,256]{1,0:T(8,128)(2,1)S(1)} %get-tuple-element.419), channel_id=1, source_target_pairs={{1,0},{2,1},{3,2},{4,3},{5,4},{6,5},{7,6},{8,7},{9,8},{10,9},{11,1... | collective-permute-start | bytes 98312 | tf_op jit(solution)/shard_map/ppermute | solution.py:16
  502.8 14.3 %collective-permute-start.6 = (bf16[64,256]{1,0:T(8,128)(2,1)S(1)}, bf16[64,256]{1,0:T(8,128)(2,1)S(1)}, u32[]{:S(2)}, u32[]{:S(2)}) collective-permute-start(bf16[64,256]{1,0:T(8,128)(2,1)S(1)} %get-tuple-element.420), channel_id=1, source_target_pairs={{0,1},{1,2},{2,3},{3,4},{4,5},{5,6},{6,7},{7,8},{8,9},{9,10},{10,1... | collective-permute-start | bytes 98312 | tf_op jit(solution)/shard_map/ppermute | solution.py:16
  506.2 9.6 %collective-permute-start.5 = (bf16[64,256]{1,0:T(8,128)(2,1)S(1)}, bf16[64,256]{1,0:T(8,128)(2,1)S(1)}, u32[]{:S(2)}, u32[]{:S(2)}) collective-permute-start(bf16[64,256]{1,0:T(8,128)(2,1)S(1)} %get-tuple-element.421), channel_id=1, source_target_pairs={{32,0},{64,32},{96,64},{33,1},{65,33},{97,65},{34,2},{66,34},{98,6... | collective-permute-start | bytes 98312 | tf_op jit(solution)/shard_map/ppermute | solution.py:16
  507.5 6.8 %collective-permute-start.4 = (bf16[64,256]{1,0:T(8,128)(2,1)S(1)}, bf16[64,256]{1,0:T(8,128)(2,1)S(1)}, u32[]{:S(2)}, u32[]{:S(2)}) collective-permute-start(bf16[64,256]{1,0:T(8,128)(2,1)S(1)} %get-tuple-element.422), channel_id=1, source_target_pairs={{0,32},{32,64},{64,96},{1,33},{33,65},{65,97},{2,34},{34,66},{66,9... | collective-permute-start | bytes 98312 | tf_op jit(solution)/shard_map/ppermute | solution.py:16
Sparse Core Ops, SparseCore 0:
  381.3 150.3 all-reduce.7
where the time goes:
time: 558 us; the launch traced here: 547 us
  other arithmetic  180 us (32%)
  local copies, waits for them, and re-layouts  133 us (24%)
  blocking collectives  81.3 us (15%)
  matrix products  51.8 us (9%)
  starting transfers between devices  48.9 us (9%)
  waiting for transfers between devices  34.8 us (6%)
  between operations  15.7 us (3%)
    scatter-add x16, other arithmetic, scatter_neighbour(): return total.at[near_tile[index]].add(spread)  105 us
    psum x1, blocking collectives, body(): lax.psum((near_grad, sums[0], sums[1], sums[2], sums[3], sums[4]), ('tx',...  81.3 us
    gather x16, local copies, waits for them, and re-layouts, add_neighbour(): jnp.take(extended, near_tile[index], axis=0).astype(jnp.float32)  63.1 us
    all_to_all x1, waiting for transfers between devices, body(): lax.all_to_all(outgoing, ('tx', 'ty'), split_axis=0, concat_axis=0, tiled...  23.7 us
    ppermute x8, starting transfers between devices, shifted(): lax.ppermute(value, axis, [(source, source + steps) for source in range(i...  22.5 us
    all_to_all x1, starting transfers between devices, body(): lax.all_to_all(outgoing, ('tx', 'ty'), split_axis=0, concat_axis=0, tiled...  22 us
    select_n x16, other arithmetic, add_neighbour(): jnp.take(extended, near_tile[index], axis=0).astype(jnp.float32)  12.4 us
    select_n x16, other arithmetic, scatter_neighbour(): return total.at[near_tile[index]].add(spread)  12.3 us
  transfers between devices with their start and end apart: 11, of which 2 were waited for; matrix products, arithmetic and copies ran while one was open for 29% of the time, Pallas kernels for 0%

commit v1 on v0

--- a/solution.py
+++ b/solution.py
@@ -264,7 +264,7 @@
     for direction in range(4):
         row_grad = row_grad.at[lists[direction]].add(came_back[direction].astype(jnp.float32))
     near_sum, gain_one_sum, conv_sum, gain_two_sum, up_sum, down_sum = lax.psum(
-        (near_grad, sums[0], sums[1], sums[2], sums[3], sums[4]), ("tx", "ty")
+        lax.psum((near_grad, sums[0], sums[1], sums[2], sums[3], sums[4]), "ty"), "tx"
     )
     totals = (gain_one_sum, conv_sum, gain_two_sum, up_sum, down_sum)
     scale = 1.0 / math.sqrt(tiles * tile_rows)

time: 558 us -> 599 us (1.073)
  waiting for transfers between devices: 34.8 us -> 85.6 us
  blocking collectives: 81.3 us -> 70.1 us
    all_to_all x1, waiting for transfers between devices: 0.01 us -> 30.6 us  [body(): lax.all_to_all(back_slots, ('tx', 'ty'), split_axis=0, concat_axis=0, til...]
    psum x1 -> x2, waiting for transfers between devices: 11 us -> 31.2 us  [the longest x1 31.2 us: body(): lax.psum((near_grad, sums[0], sums[1], sums[2], sums[3], sums[4]), 'ty')]
    psum x1 -> x2, blocking collectives: 81.3 us -> 70.1 us  [the longest x1 63.3 us: body(): lax.psum((near_grad, sums[0], sums[1], sums[2], sums[3], sums[4]), 'ty')]
  transfers between devices with their start and end apart: 11 -> 12, of which waited for: 2 -> 3; matrix products, arithmetic and copies ran while one was open for 29% -> 27% of each run, Pallas kernels for 0% -> 0%
where the time goes in v1:
time: 599 us; the launch traced here: 588 us
  other arithmetic  180 us (30%)
  local copies, waits for them, and re-layouts  133 us (22%)
  waiting for transfers between devices  85.6 us (14%)
  blocking collectives  70.1 us (12%)
  matrix products  52.8 us (9%)
  starting transfers between devices  48.6 us (8%)
  between operations  15.7 us (3%)
    scatter-add x16, other arithmetic, scatter_neighbour(): return total.at[near_tile[index]].add(spread)  105 us
    psum x1, blocking collectives, body(): lax.psum((near_grad, sums[0], sums[1], sums[2], sums[3], sums[4]), 'ty')  63.3 us
    gather x16, local copies, waits for them, and re-layouts, add_neighbour(): jnp.take(extended, near_tile[index], axis=0).astype(jnp.float32)  63.1 us
    psum x1, waiting for transfers between devices, body(): lax.psum((near_grad, sums[0], sums[1], sums[2], sums[3], sums[4]), 'ty')  31.2 us
    all_to_all x1, waiting for transfers between devices, body(): lax.all_to_all(back_slots, ('tx', 'ty'), split_axis=0, concat_axis=0, til...  30.6 us
    all_to_all x1, waiting for transfers between devices, body(): lax.all_to_all(outgoing, ('tx', 'ty'), split_axis=0, concat_axis=0, tiled...  23.8 us
    ppermute x8, starting transfers between devices, shifted(): lax.ppermute(value, axis, [(source, source + steps) for source in range(i...  22.2 us
    all_to_all x1, starting transfers between devices, body(): lax.all_to_all(outgoing, ('tx', 'ty'), split_axis=0, concat_axis=0, tiled...  22 us
  transfers between devices with their start and end apart: 12, of which 3 were waited for; matrix products, arithmetic and copies ran while one was open for 27% of the time, Pallas kernels for 0%

profile of v1, /device:TPU:1, one launch (start us, length us, event | category | flops | bytes accessed | tf_op | source)
XLA Modules:
  0.0 587.7 jit_solution(15298942087728561983)
XLA Ops:
  11.1 4.6 collective-permute-start.3
  17.6 3.5 collective-permute-start.1
  24.9 4.4 sort.17
  29.3 4.5 gather_fusion.1
  34.2 6.6 %gather_fusion.2 = s32[1024]{0:T(1024)S(1)} fusion(s32[128]{0:T(128)S(1)} %sub.18, s32[1024]{0:T(1024)S(1)} %broadcast_clamp_fusion.3), kind=kCustom, calls=%fused_computation.2 | custom fusion | bytes 12288 | tf_op jit(solution)/shard_map/jit(_take)/gather | solution.py:82
  40.8 4.3 scatter_custom_fusion.1
  49.6 81.9 %while.51 = (s32[]{:T(128)}, f32[1024,256]{1,0:T(8,128)S(1)}, s32[16,1024]{1,0:T(8,128)}, bf16[1280,256]{1,0:T(8,128)(2,1)S(1)}, s32[]{:T(128)}, /*index=5*/s32[]{:T(128)}) while((s32[]{:T(128)}, f32[1024,256]{1,0:T(8,128)S(1)}, s32[16,1024]{1,0:T(8,128)}, bf16[1280,256]{1,0:T(8,128)(2,1)S(1)}, s32[]{:T(128)}, ...), condition=%wide.region_5.6_spmd.clone, body=%wide.region_4.5_spmd.clone.sunk | while | flops 1058819 | bytes 3700827 | solution.py:43
  50.5 3.9 gather_fusion
  55.6 3.9 gather_fusion
  60.7 3.9 gather_fusion
  65.8 3.9 gather_fusion
  70.9 3.9 gather_fusion
  76.0 3.9 gather_fusion
  81.1 3.9 gather_fusion
  86.3 3.9 gather_fusion
  91.4 3.9 gather_fusion
  96.5 3.9 gather_fusion
  101.6 3.9 gather_fusion
  106.7 3.9 gather_fusion
  111.8 3.9 gather_fusion
  117.0 3.9 gather_fusion
  122.1 3.9 gather_fusion
  127.2 3.9 gather_fusion
  133.7 6.7 %scatter_custom_fusion.2 = bf16[2048,512]{1,0:T(8,128)(2,1)} fusion(s32[1024]{0:T(1024)S(1)} %get-tuple-element.414, bf16[1024,512]{1,0:T(8,128)(2,1)S(1)} %copy.65, bf16[]{:T(256)} %constant.215.clone.1), kind=kCustom, calls=%fused_computation.126 | custom fusion | bytes 2097154 | tf_op jit(solution)/shard_map/scatter | solution.py:225
  140.4 22.0 %all-to-all-start = ((bf16[128,16,512]{2,1,0:T(8,128)(2,1)}), bf16[128,16,512]{2,1,0:T(8,128)(2,1)S(1)}, u32[]{:S(2)}, u32[]{:S(2)}) async-start(bf16[128,16,512]{2,1,0:T(8,128)(2,1)} %bitcast.194), calls=%async_computation | async-start | bytes 4194304 | tf_op jit(solution)/shard_map/all_to_all | solution.py:227
  166.0 3.0 reshape.393
  169.1 23.8 %all-to-all-done = bf16[128,16,512]{2,1,0:T(8,128)(2,1)S(1)} async-done(((bf16[128,16,512]{2,1,0:T(8,128)(2,1)}), bf16[128,16,512]{2,1,0:T(8,128)(2,1)S(1)}, u32[]{:S(2)}, u32[]{:S(2)}) %all-to-all-start) | async-done | bytes 2097184 | tf_op jit(solution)/shard_map/all_to_all | solution.py:227
  192.8 9.2 %gather_fusion.4 = bf16[2048,512]{1,0:T(8,128)(2,1)} fusion(bf16[2048,512]{1,0:T(8,128)(2,1)S(1)} %bitcast.188, s32[2048]{0:T(1024)S(1)} %broadcast_clamp_fusion.1), kind=kCustom, calls=%fused_computation.4 | custom fusion | bytes 4202496 | tf_op jit(solution)/shard_map/jit(_take)/gather | solution.py:228
  202.0 3.0 copy.66
  206.6 68.3 %while.52 = (s32[]{:T(128)}, f32[256]{0:T(256)S(1)}, f32[3,8,32,32]{3,2,1,0:T(8,128)}, f32[256]{0:T(256)S(1)}, f32[256,1024]{1,0:T(8,128)}, /*index=5*/f32[1024,...) while((s32[]{:T(128)}, f32[256]{0:T(256)S(1)}, ...), condition=%wide.region_14.15_spmd.clone, body=%wide.region_7.14_spmd.clone.sunk | while | flops 4135946752 | bytes 123703776 | solution.py:244
  218.1 2.5 fusion.180
  221.9 4.9 convolution_add_fusion.11
  226.8 3.0 fusion.173
  252.1 2.5 fusion.180
  255.9 5.2 convolution_add_fusion.11
  261.1 3.0 fusion.173
  274.9 11.5 %scatter_custom_fusion.3 = bf16[2048,512]{1,0:T(8,128)(2,1)} fusion(s32[2048]{0:T(1024)} %bitcast.205, bf16[2048,256]{1,0:T(8,128)(2,1)} %bitcast.198, bf16[]{:T(256)} %constant.244, bf16[2048,256]{1,0:T(8,128)(2,1)} %bitcast.199, bf16[]{:T(256)} %constant.215.clone.1), kind=kCustom, calls=%fused_computation.105 | custom fusion | flops 4194304 | bytes 4195328 | tf_op jit(solution)/shard_map/scatter | solution.py:250
  286.4 4.4 all-to-all-start.1
  290.8 30.6 %all-to-all-done.1 = bf16[128,16,512]{2,1,0:T(8,128)(2,1)S(1)} async-done(((bf16[128,16,512]{2,1,0:T(8,128)(2,1)}), bf16[128,16,512]{2,1,0:T(8,128)(2,1)S(1)}, u32[]{:S(2)}, u32[]{:S(2)}) %all-to-all-start.1) | async-done | bytes 2097184 | tf_op jit(solution)/shard_map/all_to_all | solution.py:251
  321.4 4.0 gather_fusion.5
  329.7 63.3 %all-reduce.4 = (f32[256]{0:T(256)S(1)}, f32[256]{0:T(256)S(1)}) all-reduce(f32[256]{0:T(256)S(1)} %get-tuple-element.250, f32[256]{0:T(256)S(1)} %get-tuple-element.252), channel_id=1, replica_groups=mesh['tx'=4,'ty'=32] {'ty'}, use_global_device_ids=true, to_apply=%region_25.26 | all-reduce | flops 512 | bytes 4096 | tf_op jit(solution)/shard_map/psum | solution.py:267
  393.0 6.8 %all-reduce.6 = (f32[256]{0:T(256)S(1)}, f32[256]{0:T(256)S(1)}) all-reduce(f32[256]{0:T(256)S(1)} %get-tuple-element.399, f32[256]{0:T(256)S(1)} %get-tuple-element.400), channel_id=1, replica_groups=mesh['tx'=4,'ty'=32] {'tx'}, use_global_device_ids=true, to_apply=%region_26.27 | all-reduce | flops 512 | bytes 4096 | tf_op jit(solution)/shard_map/psum | solution.py:266
  401.8 31.2 %all-reduce.11.cloned.1.call-done = (f32[256,256]{1,0:T(8,128)}, f32[3,8,32,32]{3,2,1,0:T(8,128)}, f32[256,1024]{1,0:T(8,128)}, f32[1024,256]{1,0:T(8,128)}) async-done(((f32[256,256]{1,0:T(8,128)}, f32[3,8,32,32]{3,2,1,0:T(8,128)}, f32[256,1024]{1,0:T(8,128)}, f32[1024,256]{1,0:T(8,128)}), (f32[256,256]{1,0:T(8,128)}, f32[3,8,32,32]{3,2,1,0:T(8,128)}, f32[256,1024]{1,0:T(8,128)}, ...) | async-done | bytes 2457616 | tf_op jit(solution)/shard_map/psum | solution.py:267
  433.1 117.5 %while.50 = (s32[]{:T(128)}, f32[1280,256]{1,0:T(8,128)S(1)}, s32[16,1024]{1,0:T(8,128)}, f32[1024,256]{1,0:T(8,128)S(1)}, s32[]{:T(128)}) while((s32[]{:T(128)}, f32[1280,256]{1,0:T(8,128)S(1)}, s32[16,1024]{1,0:T(8,128)}, f32[1024,256]{1,0:T(8,128)S(1)}, s32[]{:T(128)}) %tuple.124), condition=%wide.region_18.19_spmd, body=%wide.region_16.18_spmd.sunk | while | flops 265218 | bytes 3158089 | solution.py:64
  433.9 6.5 %scatter_fusion = f32[1280,256]{1,0:T(8,128)S(1)} fusion(f32[1280,256]{1,0:T(8,128)S(1)} %get-tuple-element.685, s32[1024]{0:T(1024)S(1)} %bitcast.200, f32[1024,256]{1,0:T(8,128)S(1)} %get-tuple-element.692), kind=kCustom, calls=%fused_computation.6.clone.1 | custom fusion | flops 262144 | bytes 3149824 | tf_op jit(solution)/shard_map/while/body/eval_jaxpr/scatter-add | solution.py:62
  441.3 6.5 %scatter_fusion = f32[1280,256]{1,0:T(8,128)S(1)} fusion(f32[1280,256]{1,0:T(8,128)S(1)} %get-tuple-element.685, s32[1024]{0:T(1024)S(1)} %bitcast.200, f32[1024,256]{1,0:T(8,128)S(1)} %get-tuple-element.692), kind=kCustom, calls=%fused_computation.6.clone.1 | custom fusion | flops 262144 | bytes 3149824 | tf_op jit(solution)/shard_map/while/body/eval_jaxpr/scatter-add | solution.py:62
  448.6 6.5 %scatter_fusion = f32[1280,256]{1,0:T(8,128)S(1)} fusion(f32[1280,256]{1,0:T(8,128)S(1)} %get-tuple-element.685, s32[1024]{0:T(1024)S(1)} %bitcast.200, f32[1024,256]{1,0:T(8,128)S(1)} %get-tuple-element.692), kind=kCustom, calls=%fused_computation.6.clone.1 | custom fusion | flops 262144 | bytes 3149824 | tf_op jit(solution)/shard_map/while/body/eval_jaxpr/scatter-add | solution.py:62
  456.0 6.5 %scatter_fusion = f32[1280,256]{1,0:T(8,128)S(1)} fusion(f32[1280,256]{1,0:T(8,128)S(1)} %get-tuple-element.685, s32[1024]{0:T(1024)S(1)} %bitcast.200, f32[1024,256]{1,0:T(8,128)S(1)} %get-tuple-element.692), kind=kCustom, calls=%fused_computation.6.clone.1 | custom fusion | flops 262144 | bytes 3149824 | tf_op jit(solution)/shard_map/while/body/eval_jaxpr/scatter-add | solution.py:62
  463.3 6.5 %scatter_fusion = f32[1280,256]{1,0:T(8,128)S(1)} fusion(f32[1280,256]{1,0:T(8,128)S(1)} %get-tuple-element.685, s32[1024]{0:T(1024)S(1)} %bitcast.200, f32[1024,256]{1,0:T(8,128)S(1)} %get-tuple-element.692), kind=kCustom, calls=%fused_computation.6.clone.1 | custom fusion | flops 262144 | bytes 3149824 | tf_op jit(solution)/shard_map/while/body/eval_jaxpr/scatter-add | solution.py:62
  470.6 6.5 %scatter_fusion = f32[1280,256]{1,0:T(8,128)S(1)} fusion(f32[1280,256]{1,0:T(8,128)S(1)} %get-tuple-element.685, s32[1024]{0:T(1024)S(1)} %bitcast.200, f32[1024,256]{1,0:T(8,128)S(1)} %get-tuple-element.692), kind=kCustom, calls=%fused_computation.6.clone.1 | custom fusion | flops 262144 | bytes 3149824 | tf_op jit(solution)/shard_map/while/body/eval_jaxpr/scatter-add | solution.py:62
  478.0 6.5 %scatter_fusion = f32[1280,256]{1,0:T(8,128)S(1)} fusion(f32[1280,256]{1,0:T(8,128)S(1)} %get-tuple-element.685, s32[1024]{0:T(1024)S(1)} %bitcast.200, f32[1024,256]{1,0:T(8,128)S(1)} %get-tuple-element.692), kind=kCustom, calls=%fused_computation.6.clone.1 | custom fusion | flops 262144 | bytes 3149824 | tf_op jit(solution)/shard_map/while/body/eval_jaxpr/scatter-add | solution.py:62
  485.3 6.5 %scatter_fusion = f32[1280,256]{1,0:T(8,128)S(1)} fusion(f32[1280,256]{1,0:T(8,128)S(1)} %get-tuple-element.685, s32[1024]{0:T(1024)S(1)} %bitcast.200, f32[1024,256]{1,0:T(8,128)S(1)} %get-tuple-element.692), kind=kCustom, calls=%fused_computation.6.clone.1 | custom fusion | flops 262144 | bytes 3149824 | tf_op jit(solution)/shard_map/while/body/eval_jaxpr/scatter-add | solution.py:62
  492.7 6.5 %scatter_fusion = f32[1280,256]{1,0:T(8,128)S(1)} fusion(f32[1280,256]{1,0:T(8,128)S(1)} %get-tuple-element.685, s32[1024]{0:T(1024)S(1)} %bitcast.200, f32[1024,256]{1,0:T(8,128)S(1)} %get-tuple-element.692), kind=kCustom, calls=%fused_computation.6.clone.1 | custom fusion | flops 262144 | bytes 3149824 | tf_op jit(solution)/shard_map/while/body/eval_jaxpr/scatter-add | solution.py:62
  500.0 6.5 %scatter_fusion = f32[1280,256]{1,0:T(8,128)S(1)} fusion(f32[1280,256]{1,0:T(8,128)S(1)} %get-tuple-element.685, s32[1024]{0:T(1024)S(1)} %bitcast.200, f32[1024,256]{1,0:T(8,128)S(1)} %get-tuple-element.692), kind=kCustom, calls=%fused_computation.6.clone.1 | custom fusion | flops 262144 | bytes 3149824 | tf_op jit(solution)/shard_map/while/body/eval_jaxpr/scatter-add | solution.py:62
  507.4 6.5 %scatter_fusion = f32[1280,256]{1,0:T(8,128)S(1)} fusion(f32[1280,256]{1,0:T(8,128)S(1)} %get-tuple-element.685, s32[1024]{0:T(1024)S(1)} %bitcast.200, f32[1024,256]{1,0:T(8,128)S(1)} %get-tuple-element.692), kind=kCustom, calls=%fused_computation.6.clone.1 | custom fusion | flops 262144 | bytes 3149824 | tf_op jit(solution)/shard_map/while/body/eval_jaxpr/scatter-add | solution.py:62
  514.7 6.5 %scatter_fusion = f32[1280,256]{1,0:T(8,128)S(1)} fusion(f32[1280,256]{1,0:T(8,128)S(1)} %get-tuple-element.685, s32[1024]{0:T(1024)S(1)} %bitcast.200, f32[1024,256]{1,0:T(8,128)S(1)} %get-tuple-element.692), kind=kCustom, calls=%fused_computation.6.clone.1 | custom fusion | flops 262144 | bytes 3149824 | tf_op jit(solution)/shard_map/while/body/eval_jaxpr/scatter-add | solution.py:62
  522.0 6.5 %scatter_fusion = f32[1280,256]{1,0:T(8,128)S(1)} fusion(f32[1280,256]{1,0:T(8,128)S(1)} %get-tuple-element.685, s32[1024]{0:T(1024)S(1)} %bitcast.200, f32[1024,256]{1,0:T(8,128)S(1)} %get-tuple-element.692), kind=kCustom, calls=%fused_computation.6.clone.1 | custom fusion | flops 262144 | bytes 3149824 | tf_op jit(solution)/shard_map/while/body/eval_jaxpr/scatter-add | solution.py:62
  529.4 6.5 %scatter_fusion = f32[1280,256]{1,0:T(8,128)S(1)} fusion(f32[1280,256]{1,0:T(8,128)S(1)} %get-tuple-element.685, s32[1024]{0:T(1024)S(1)} %bitcast.200, f32[1024,256]{1,0:T(8,128)S(1)} %get-tuple-element.692), kind=kCustom, calls=%fused_computation.6.clone.1 | custom fusion | flops 262144 | bytes 3149824 | tf_op jit(solution)/shard_map/while/body/eval_jaxpr/scatter-add | solution.py:62
  536.7 6.5 %scatter_fusion = f32[1280,256]{1,0:T(8,128)S(1)} fusion(f32[1280,256]{1,0:T(8,128)S(1)} %get-tuple-element.685, s32[1024]{0:T(1024)S(1)} %bitcast.200, f32[1024,256]{1,0:T(8,128)S(1)} %get-tuple-element.692), kind=kCustom, calls=%fused_computation.6.clone.1 | custom fusion | flops 262144 | bytes 3149824 | tf_op jit(solution)/shard_map/while/body/eval_jaxpr/scatter-add | solution.py:62
  544.1 6.5 %scatter_fusion = f32[1280,256]{1,0:T(8,128)S(1)} fusion(f32[1280,256]{1,0:T(8,128)S(1)} %get-tuple-element.685, s32[1024]{0:T(1024)S(1)} %bitcast.200, f32[1024,256]{1,0:T(8,128)S(1)} %get-tuple-element.692), kind=kCustom, calls=%fused_computation.6.clone.1 | custom fusion | flops 262144 | bytes 3149824 | tf_op jit(solution)/shard_map/while/body/eval_jaxpr/scatter-add | solution.py:62
  552.2 2.8 collective-permute-start.7
  555.0 2.8 collective-permute-start.6
  559.1 4.0 collective-permute-start.4
  575.8 2.3 broadcast_multiply_fusion.3
  (303 shorter events, 122.1 us)
Async XLA Ops:
  7.2 124.3 %copy-start = (bf16[256,256]{1,0:T(8,128)(2,1)S(1)}, bf16[256,256]{1,0:T(8,128)(2,1)}, u32[]{:S(2)}) copy-start(bf16[256,256]{1,0:T(8,128)(2,1)} %param.25) | copy-start | bytes 393220
  7.2 22.1 %copy-start.1 = (s32[1,1024]{1,0:T(1,128)S(1)}, s32[1,1024]{1,0:T(1,128)}, u32[]{:S(2)}) copy-start(s32[1,1024]{1,0:T(1,128)} %param.21) | copy-start | bytes 12292
  11.1 35.9 %collective-permute-start.3 = (bf16[64,256]{0,1:T(8,128)(2,1)S(1)}, bf16[64,256]{0,1:T(8,128)(2,1)S(1)}, u32[]{:S(2)}, u32[]{:S(2)}) collective-permute-start(bf16[64,256]{0,1:T(8,128)(2,1)S(1)} %get-tuple-element.429), channel_id=1, source_target_pairs={{0,1},{1,2},{2,3},{3,4},{4,5},{5,6},{6,7},{7,8},{8,9},{9,10},{10,1... | collective-permute-start | bytes 98312 | tf_op jit(solution)/shard_map/ppermute | solution.py:16
  15.7 31.3 %collective-permute-start.2 = (bf16[64,256]{0,1:T(8,128)(2,1)S(1)}, bf16[64,256]{0,1:T(8,128)(2,1)S(1)}, u32[]{:S(2)}, u32[]{:S(2)}) collective-permute-start(bf16[64,256]{0,1:T(8,128)(2,1)S(1)} %get-tuple-element.430), channel_id=1, source_target_pairs={{1,0},{2,1},{3,2},{4,3},{5,4},{6,5},{7,6},{8,7},{9,8},{10,9},{11,1... | collective-permute-start | bytes 98312 | tf_op jit(solution)/shard_map/ppermute | solution.py:16
  17.6 29.4 %collective-permute-start.1 = (bf16[64,256]{0,1:T(8,128)(2,1)S(1)}, bf16[64,256]{0,1:T(8,128)(2,1)S(1)}, u32[]{:S(2)}, u32[]{:S(2)}) collective-permute-start(bf16[64,256]{0,1:T(8,128)(2,1)S(1)} %get-tuple-element.431), channel_id=1, source_target_pairs={{0,32},{32,64},{64,96},{1,33},{33,65},{65,97},{2,34},{34,66},{66,9... | collective-permute-start | bytes 98312 | tf_op jit(solution)/shard_map/ppermute | solution.py:16
  21.2 25.8 %collective-permute-start = (bf16[64,256]{0,1:T(8,128)(2,1)S(1)}, bf16[64,256]{0,1:T(8,128)(2,1)S(1)}, u32[]{:S(2)}, u32[]{:S(2)}) collective-permute-start(bf16[64,256]{0,1:T(8,128)(2,1)S(1)} %get-tuple-element.432), channel_id=1, source_target_pairs={{32,0},{64,32},{96,64},{33,1},{65,33},{97,65},{34,2},{66,34},{98,6... | collective-permute-start | bytes 98312 | tf_op jit(solution)/shard_map/ppermute | solution.py:16
  29.3 16.5 %copy-start.12 = (bf16[1,1024,256]{2,1,0:T(8,128)(2,1)S(1)}, bf16[1,1024,256]{2,1,0:T(8,128)(2,1)}, u32[]{:S(2)}) copy-start(bf16[1,1024,256]{2,1,0:T(8,128)(2,1)} %param.19) | copy-start | bytes 1572868
  29.3 16.7 %copy-start.15 = (bf16[1,1024,256]{2,1,0:T(8,128)(2,1)S(1)}, bf16[1,1024,256]{2,1,0:T(8,128)(2,1)}, u32[]{:S(2)}) copy-start(bf16[1,1024,256]{2,1,0:T(8,128)(2,1)} %param.31) | copy-start | bytes 1572868
  45.7 87.9 %copy-start.25 = (s32[1024]{0:T(1024)}, s32[1024]{0:T(1024)S(1)}, u32[]{:S(2)}) copy-start(s32[1024]{0:T(1024)S(1)} %get-tuple-element.414) | copy-start | bytes 12292
  47.0 0.6 copy-start.18
  47.0 0.6 copy-start.19
  47.0 0.6 copy-start.20
  47.6 0.6 copy-start.21
  49.6 83.5 %copy-start.14 = (bf16[1,1024,256]{1,2,0:T(8,128)(2,1)S(1)}, bf16[1,1024,256]{1,2,0:T(8,128)(2,1)}, u32[]{:S(2)}) copy-start(bf16[1,1024,256]{1,2,0:T(8,128)(2,1)} %copy.64) | copy-start | bytes 1572868
  131.5 8.9 %copy-start.6 = (f32[1024,256]{1,0:T(8,128)}, f32[1024,256]{1,0:T(8,128)S(1)}, u32[]{:S(2)}) copy-start(f32[1024,256]{1,0:T(8,128)S(1)} %get-tuple-element.246) | copy-start | bytes 3145732
  133.1 29.9 %copy-start.22 = (s32[1,2048]{1,0:T(1,128)S(1)}, s32[1,2048]{1,0:T(1,128)}, u32[]{:S(2)}) copy-start(s32[1,2048]{1,0:T(1,128)} %param.22) | copy-start | bytes 24580
  140.4 52.4 %all-to-all-start = ((bf16[128,16,512]{2,1,0:T(8,128)(2,1)}), bf16[128,16,512]{2,1,0:T(8,128)(2,1)S(1)}, u32[]{:S(2)}, u32[]{:S(2)}) async-start(bf16[128,16,512]{2,1,0:T(8,128)(2,1)} %bitcast.194), calls=%async_computation | async-start | bytes 4194304 | tf_op jit(solution)/shard_map/all_to_all | solution.py:227
  169.0 33.0 %copy-start.23 = (s32[2048,1]{0,1:T(1,128)}, s32[2048,1]{0,1:T(1,128)S(1)}, u32[]{:S(2)}) copy-start(s32[2048,1]{0,1:T(1,128)S(1)} %compare_select_fusion.3) | copy-start | bytes 24580
  202.0 4.6 copy-start.16
  202.0 4.6 copy-start.17
  213.4 4.7 copy-start.28
  216.1 1.9 copy-start.2
  221.9 4.9 copy-start.3
  221.9 4.9 copy-start.29
  229.8 2.1 copy-start.8
  231.9 1.3 copy-start.4
  231.9 1.9 copy-start.5
  232.9 3.0 copy-start.9
  232.9 1.3 copy-start.10
  234.3 4.3 copy-start.11
  247.4 4.7 copy-start.28
  250.1 1.9 copy-start.2
  255.9 5.2 copy-start.3
  255.9 5.2 copy-start.29
  264.1 2.1 copy-start.8
  266.2 1.3 copy-start.4
  266.2 1.9 copy-start.5
  267.2 3.0 copy-start.9
  267.2 1.3 copy-start.10
  268.6 4.3 copy-start.11
  274.9 15.9 %copy-start.26 = (s32[1024]{0:T(1024)S(1)}, s32[1024]{0:T(1024)}, u32[]{:S(2)}) copy-start(s32[1024]{0:T(1024)} %copy-done.25) | copy-start | bytes 12292
  286.4 35.0 %all-to-all-start.1 = ((bf16[128,16,512]{2,1,0:T(8,128)(2,1)}), bf16[128,16,512]{2,1,0:T(8,128)(2,1)S(1)}, u32[]{:S(2)}, u32[]{:S(2)}) async-start(bf16[128,16,512]{2,1,0:T(8,128)(2,1)} %bitcast.193), calls=%async_computation.1 | async-start | bytes 4194304 | tf_op jit(solution)/shard_map/all_to_all | solution.py:251
  290.8 142.3 %all-reduce.11.cloned.1.call-start = ((), (), s32[]{:S(2)}) async-start(), calls=%async_computation.2 | async-start | bytes 5505024 | tf_op jit(solution)/shard_map/psum | solution.py:267
  321.4 4.5 copy-start.27
  325.4 2.6 copy-start.7
  326.0 3.2 copy-start.24
  328.0 71.8 %copy-start.13 = (bf16[1024,256]{0,1:T(8,128)(2,1)}, bf16[1024,256]{0,1:T(8,128)(2,1)S(1)}, u32[]{:S(2)}) copy-start(bf16[1024,256]{0,1:T(8,128)(2,1)S(1)} %fusion.57) | copy-start | bytes 1572868
  329.1 243.3 %all-reduce.13.cloned.1.call-start = ((), (), s32[]{:S(2)}) async-start(), calls=%async_computation.3 | async-start | bytes 5505024 | tf_op jit(solution)/shard_map/psum | solution.py:266
  552.2 18.0 %collective-permute-start.7 = (bf16[64,256]{1,0:T(8,128)(2,1)S(1)}, bf16[64,256]{1,0:T(8,128)(2,1)S(1)}, u32[]{:S(2)}, u32[]{:S(2)}) collective-permute-start(bf16[64,256]{1,0:T(8,128)(2,1)S(1)} %get-tuple-element.425), channel_id=1, source_target_pairs={{1,0},{2,1},{3,2},{4,3},{5,4},{6,5},{7,6},{8,7},{9,8},{10,9},{11,1... | collective-permute-start | bytes 98312 | tf_op jit(solution)/shard_map/ppermute | solution.py:16
  555.0 13.8 %collective-permute-start.6 = (bf16[64,256]{1,0:T(8,128)(2,1)S(1)}, bf16[64,256]{1,0:T(8,128)(2,1)S(1)}, u32[]{:S(2)}, u32[]{:S(2)}) collective-permute-start(bf16[64,256]{1,0:T(8,128)(2,1)S(1)} %get-tuple-element.426), channel_id=1, source_target_pairs={{0,1},{1,2},{2,3},{3,4},{4,5},{5,6},{6,7},{7,8},{8,9},{9,10},{10,1... | collective-permute-start | bytes 98312 | tf_op jit(solution)/shard_map/ppermute | solution.py:16
  557.8 9.5 %collective-permute-start.5 = (bf16[64,256]{1,0:T(8,128)(2,1)S(1)}, bf16[64,256]{1,0:T(8,128)(2,1)S(1)}, u32[]{:S(2)}, u32[]{:S(2)}) collective-permute-start(bf16[64,256]{1,0:T(8,128)(2,1)S(1)} %get-tuple-element.427), channel_id=1, source_target_pairs={{32,0},{64,32},{96,64},{33,1},{65,33},{97,65},{34,2},{66,34},{98,6... | collective-permute-start | bytes 98312 | tf_op jit(solution)/shard_map/ppermute | solution.py:16
  559.1 6.7 %collective-permute-start.4 = (bf16[64,256]{1,0:T(8,128)(2,1)S(1)}, bf16[64,256]{1,0:T(8,128)(2,1)S(1)}, u32[]{:S(2)}, u32[]{:S(2)}) collective-permute-start(bf16[64,256]{1,0:T(8,128)(2,1)S(1)} %get-tuple-element.428), channel_id=1, source_target_pairs={{0,32},{32,64},{64,96},{1,33},{33,65},{65,97},{2,34},{34,66},{66,9... | collective-permute-start | bytes 98312 | tf_op jit(solution)/shard_map/ppermute | solution.py:16
Sparse Core Ops, SparseCore 0:
  329.2 103.7 all-reduce.10
  435.8 70.0 all-reduce.12
